TPU v7x, 256 devices: a whole 4x4x8 slice. The times are simulated.
256 devices in a mesh: dp: 64 (over y, z, core), rep: 4 (over x).
Axes of the slice: x: 4, y: 4, z: 8, core: 2. Of those that a mesh axis runs over, the one named last changes fastest.
Arguments:
- item_table: bfloat16 [32768, 512], P(('dp', 'rep')), may hold values from -6 to 6
- requests: int32 [256, 256, 2], P(('dp', 'rep')), may hold values from 0 to 127, as said below
- event_slot: int32 [131072], P(('dp', 'rep')), may hold values from 0 to 511, as said below
- lengths: int32 [256, 4], P(('dp', 'rep')), may hold values from 1 to 256, 512 in all within a row
- leaf_ids: int32 [131072, 8], P(('dp', 'rep')), may hold values from 0 to 31
- leaf_table: bfloat16 [256, 512], replicated, may hold values from -2.09375 to 2.09375
- w_in: bfloat16 [512, 2048], replicated, may hold values from -0.25 to 0.25
- w_out: bfloat16 [512, 512], replicated, may hold values from -0.25 to 0.25
- cotangent: bfloat16 [131072, 512], P(('dp', 'rep')), may hold values from -6 to 6
Outputs:
- output: bfloat16 [131072, 512], P(('dp', 'rep'))
- table_grad: float32 [32768, 512], P(('dp', 'rep'))
- leaf_grad: float32 [256, 512], replicated
- w_in_grad: float32 [512, 2048], replicated
- w_out_grad: float32 [512, 512], replicated
Inputs may be any that keep to these rules, and one draw needn't show every extreme that they name: `requests`: for each device and owner the 2 requested rows are distinct. `event_slot`: every one of a device's 512 slots is named by at least one of its events.
All inputs are finite; a program needn't handle non-finite values.
Results may differ from a plain program's by a relative error of at most 0.014.
Values may be sent and summed in bfloat16 or wider, within the bound.
A program may use at most 64 MiB of HBM per device.

v0:
```python
import jax
import jax.numpy as jnp
from jax import lax
from jax.sharding import PartitionSpec as P

HEADS = 4
epsilon = 1e-06


def normalize(values):
    center = values - jnp.mean(values, axis=-1, keepdims=True)
    spread = jnp.mean(center * center, axis=-1, keepdims=True)
    return center * lax.rsqrt(spread + epsilon)


def visible(lengths, count):
    ends = jnp.cumsum(lengths)
    places = jnp.arange(count, dtype=jnp.int32)
    segment = jnp.sum((places[:, None] >= ends[None, :]).astype(jnp.int32), axis=1)
    same = segment[:, None] == segment[None, :]
    return jnp.logical_and(same, places[None, :] <= places[:, None])


def front(rows, event_slot, lengths, leaf_ids, leaf_table, w_in):
    count = event_slot.shape[0]
    picker = (event_slot[:, None] == jnp.arange(rows.shape[0], dtype=jnp.int32)[None, :]).astype(
        jnp.bfloat16
    )
    leaves = leaf_table.shape[0] // leaf_ids.shape[1]
    onehot = (
        (leaf_ids[:, :, None] == jnp.arange(leaves, dtype=jnp.int32)[None, None, :])
        .reshape(count, -1)
        .astype(jnp.bfloat16)
    )
    inputs = (
        jnp.dot(picker, rows, preferred_element_type=jnp.float32)
        + jnp.dot(onehot, leaf_table, preferred_element_type=jnp.float32)
    ).astype(jnp.bfloat16)
    normed = normalize(inputs.astype(jnp.float32)).astype(jnp.bfloat16)
    hidden = jax.nn.silu(jnp.dot(normed, w_in, preferred_element_type=jnp.float32)).astype(
        jnp.bfloat16
    )
    width = w_in.shape[0]
    head_size = width // HEADS
    gates = hidden[:, 0:width]
    value_heads = hidden[:, width : 2 * width].reshape(count, HEADS, head_size)
    query_heads = hidden[:, 2 * width : 3 * width].reshape(count, HEADS, head_size)
    key_heads = hidden[:, 3 * width : 4 * width].reshape(count, HEADS, head_size)
    scores = jnp.einsum(
        "qhd,khd->hqk", query_heads, key_heads, preferred_element_type=jnp.float32
    ) * head_size ** (-0.5)
    allowed = visible(lengths, count)
    weights = jnp.where(allowed[None], jax.nn.silu(scores), 0.0).astype(jnp.bfloat16)
    mixed = jnp.einsum(
        "hqk,khd->qhd", weights, value_heads, preferred_element_type=jnp.float32
    ).reshape(count, width)
    gated = (normalize(mixed) * gates.astype(jnp.float32)).astype(jnp.bfloat16)
    return (inputs, gated)


def back(inputs, gated, w_out):
    return (
        jnp.dot(gated, w_out, preferred_element_type=jnp.float32) + inputs.astype(jnp.float32)
    ).astype(jnp.bfloat16)


def send_asked(wanted):
    result = lax.all_to_all(
        lax.all_to_all(wanted, "dp", split_axis=0, concat_axis=0, tiled=True),
        "rep",
        split_axis=1,
        concat_axis=1,
        tiled=True,
    )
    return result


def send_fetched(fetched):
    result = lax.all_to_all(
        lax.all_to_all(fetched, "dp", split_axis=0, concat_axis=0, tiled=True),
        "rep",
        split_axis=1,
        concat_axis=1,
        tiled=True,
    )
    return result


def send_returned(gradients):
    result = lax.all_to_all(
        lax.all_to_all(gradients, "dp", split_axis=0, concat_axis=0, tiled=True),
        "rep",
        split_axis=1,
        concat_axis=1,
        tiled=True,
    )
    return result


def on_device(
    item_table, requests, event_slot, lengths, leaf_ids, leaf_table, w_in, w_out, cotangent
):
    data_count = lax.axis_size("dp")
    replica_count = lax.axis_size("rep")
    width = item_table.shape[1]
    wanted = requests.reshape(data_count, replica_count, -1)
    asked = send_asked(wanted)
    fetched = item_table[asked]
    arrived = send_fetched(fetched).reshape(-1, width)

    def local_front(rows, table_leaf, weight_in):
        return front(rows, event_slot, lengths[0], leaf_ids, table_leaf, weight_in)

    (inputs, gated), pull_front = jax.vjp(local_front, arrived, leaf_table, w_in)
    output, pull_back = jax.vjp(back, inputs, gated, w_out)
    d_inputs, d_gated, d_out = pull_back(cotangent)
    d_rows, d_leaf, d_in = pull_front((d_inputs, d_gated))
    returned = send_returned(d_rows.reshape(data_count, replica_count, -1, width))
    leaf_sum, in_sum, out_sum = lax.psum(
        (d_leaf.astype(jnp.float32), d_in.astype(jnp.float32), d_out.astype(jnp.float32)),
        ("dp", "rep"),
    )
    table_grad = (
        jnp.zeros(item_table.shape, jnp.float32)
        .at[asked.reshape(-1)]
        .add(returned.reshape(-1, width).astype(jnp.float32))
    )
    share = 1.0 / (data_count * replica_count)
    return (output, table_grad, leaf_sum * share, in_sum * share, out_sum * share)


def solution(mesh):
    return jax.shard_map(
        on_device,
        mesh=mesh,
        in_specs=(
            P(("dp", "rep"), None),
            P(("dp", "rep"), None, None),
            P(("dp", "rep")),
            P(("dp", "rep"), None),
            P(("dp", "rep"), None),
            P(),
            P(),
            P(),
            P(("dp", "rep"), None),
        ),
        out_specs=(P(("dp", "rep"), None), P(("dp", "rep"), None), P(), P(), P()),
        check_vma=False,
    )
```

profile of v0, /device:TPU:97, one launch (start us, length us, event | category | flops | bytes accessed | tf_op | source)
XLA Modules:
  0.0 433.1 jit_solution(8049075674224172676)
XLA Ops:
  8.2 18.3 %all_to_all.30 = s32[64,4,2]{1,2,0:T(2,128)S(1)} all-to-all(s32[64,4,2]{1,2,0:T(2,128)S(1)} %copy.143), channel_id=1, replica_groups=mesh['dp'=64,'rep'=4] {'dp'}, dimensions={0} | all-to-all | bytes 4096 | tf_op jit(solution)/shard_map/all_to_all | solution.py:69
  26.7 7.9 %all_to_all.31 = s32[4,1,128]{2,1,0:T(1,128)S(1)} all-to-all(s32[4,1,128]{2,1,0:T(1,128)S(1)} %reshape.234), channel_id=1, replica_groups=mesh['dp'=64,'rep'=4] {'rep'}, dimensions={0} | all-to-all | bytes 4096 | tf_op jit(solution)/shard_map/all_to_all | solution.py:68
  36.2 2.9 gather_fusion
  40.1 8.5 %all-to-all-start.2 = ((bf16[64,4,2,512]{3,2,1,0:T(2,128)(2,1)}), bf16[64,4,2,512]{3,2,1,0:T(2,128)(2,1)S(1)}, u32[]{:S(2)}, u32[]{:S(2)}) async-start(bf16[64,4,2,512]{3,2,1,0:T(2,128)(2,1)} %reshape.215), calls=%async_computation.2 | async-start | bytes 1048576 | tf_op jit(solution)/shard_map/all_to_all | solution.py:80
  50.1 15.3 %all-to-all-done.2 = bf16[64,4,2,512]{3,2,1,0:T(2,128)(2,1)S(1)} async-done(((bf16[64,4,2,512]{3,2,1,0:T(2,128)(2,1)}), bf16[64,4,2,512]{3,2,1,0:T(2,128)(2,1)S(1)}, u32[]{:S(2)}, u32[]{:S(2)}) %all-to-all-start.2) | async-done | bytes 524320 | tf_op jit(solution)/shard_map/all_to_all | solution.py:80
  66.6 3.5 all-to-all-start.3
  70.5 2.3 fusion.42
  72.8 7.3 %all-to-all-done.3 = bf16[64,4,2,512]{3,2,0,1:T(2,128)(2,1)S(1)} async-done(((bf16[64,4,2,512]{3,2,0,1:T(2,128)(2,1)}), bf16[64,4,2,512]{3,2,0,1:T(2,128)(2,1)S(1)}, u32[]{:S(2)}, u32[]{:S(2)}) %all-to-all-start.3) | async-done | bytes 524320 | tf_op jit(solution)/shard_map/all_to_all | solution.py:79
  83.2 2.0 convert_reduce_fusion
  86.0 3.9 multiply_convert_fusion
  92.4 2.1 copy.176
  96.5 4.8 %select_convert_fusion = (bf16[4,512,512]{2,1,0:T(8,128)(2,1)S(1)}, f32[4,512,512]{2,1,0:T(8,128)}) fusion(pred[512,512]{1,0:T(8,128)(4,1)S(1)} %fusion.22, bf16[512,4,128]{0,2,1:T(8,128)(2,1)} %bitcast.68, bf16[512,4,128]{0,2,1:T(8,128)(2,1)} %bitcast.70), kind=kOutput, calls=%fused_computation.11 | convolution fusion | flops 275775488 | bytes 7602176 | tf_op jit(solution)/shard_map/jvp(qhd,khd->hqk)/dot_general | solution.py:49
  103.9 2.6 copy.171
  106.5 2.1 multiply_reduce_fusion
  109.3 3.0 fusion.40
  113.2 2.1 copy.172
  115.3 5.1 %fusion.4 = bf16[4,512,512]{2,1,0:T(8,128)(2,1)S(1)} fusion(f32[4,512,512]{2,1,0:T(8,128)} %get-tuple-element.57, pred[512,512]{1,0:T(8,128)(4,1)S(1)} %fusion.22, bf16[4,128,512]{2,1,0:T(8,128)(2,1)} %bitcast.72, bf16[64,4,8,128]{3,2,1,0:T(8,128)(2,1)} %get-tuple-element.46), kind=kOutput, calls=%fused_computation.10 | convolution fusion | flops 283115520 | bytes 7602176 | tf_op jit(solution)/shard_map/transpose(jvp(hqk,khd->qhd))/dot_general | solution.py:54
  124.7 2.1 copy.173
  128.8 2.1 copy.175
  130.9 3.6 fusion
  134.5 3.3 fusion.5
  143.3 2.5 convolution_convert_fusion.1
  147.9 6.8 %all-to-all-start.4 = ((bf16[64,4,2,512]{3,2,1,0:T(2,128)(2,1)}), bf16[64,4,2,512]{3,2,1,0:T(2,128)(2,1)}, u32[]{:S(2)}, u32[]{:S(2)}) async-start(bf16[64,4,2,512]{3,2,1,0:T(2,128)(2,1)} %reshape.212), calls=%async_computation.4 | async-start | bytes 1048576 | tf_op jit(solution)/shard_map/all_to_all | solution.py:91
  155.0 17.6 %all-to-all-done.4 = bf16[64,4,2,512]{3,2,1,0:T(2,128)(2,1)} async-done(((bf16[64,4,2,512]{3,2,1,0:T(2,128)(2,1)}), bf16[64,4,2,512]{3,2,1,0:T(2,128)(2,1)}, u32[]{:S(2)}, u32[]{:S(2)}) %all-to-all-start.4) | async-done | bytes 524320 | tf_op jit(solution)/shard_map/all_to_all | solution.py:91
  172.6 2.2 copy.164
  174.8 4.4 %all-to-all-start.5 = ((bf16[64,4,2,512]{3,2,0,1:T(2,128)(2,1)}), bf16[64,4,2,512]{3,2,0,1:T(2,128)(2,1)}, u32[]{:S(2)}, u32[]{:S(2)}) async-start(bf16[64,4,2,512]{3,2,0,1:T(2,128)(2,1)} %copy.164), calls=%async_computation.5 | async-start | bytes 1048576 | tf_op jit(solution)/shard_map/all_to_all | solution.py:90
  179.2 2.3 fusion.11
  181.6 2.1 copy.167
  183.6 5.3 %all-to-all-done.5 = bf16[64,4,2,512]{3,2,0,1:T(2,128)(2,1)} async-done(((bf16[64,4,2,512]{3,2,0,1:T(2,128)(2,1)}), bf16[64,4,2,512]{3,2,0,1:T(2,128)(2,1)}, u32[]{:S(2)}, u32[]{:S(2)}) %all-to-all-start.5) | async-done | bytes 524320 | tf_op jit(solution)/shard_map/all_to_all | solution.py:90
  192.6 4.9 %scatter_custom_fusion = f32[128,512]{1,0:T(8,128)} fusion(s32[512]{0:T(512)S(1)} %bitcast.79, f32[512,512]{1,0:T(8,128)} %reshape.226, f32[]{:T(128)} %constant.15.clone.1), kind=kCustom, calls=%fused_computation.74 | custom fusion | flops 262144 | bytes 262656 | tf_op jit(solution)/shard_map/scatter-add | solution.py:126
  197.6 221.8 %all-reduce.7.cloned.1.call-done = (f32[256,512]{1,0:T(8,128)}, f32[512,2048]{1,0:T(8,128)}, f32[512,512]{1,0:T(8,128)}) async-done(((f32[256,512]{1,0:T(8,128)}, f32[512,2048]{1,0:T(8,128)}, f32[512,512]{1,0:T(8,128)}), (f32[256,512]{1,0:T(8,128)}, f32[512,2048]{1,0:T(8,128)}, f32[512,512]{1,0:T(8,128)})) %all-reduce.7.cloned.1.call-update) | async-done | bytes 5767184 | tf_op jit(solution)/shard_map/psum | solution.py:119
  419.4 4.9 %broadcast_multiply_fusion = f32[512,2048]{1,0:T(8,128)} fusion(f32[512,2048]{1,0:T(8,128)} %get-tuple-element.41), kind=kLoop, calls=%fused_computation.17 | loop fusion | flops 1048576 | bytes 8388608 | tf_op jit(solution)/shard_map/mul | solution.py:129
  (99 shorter events, 39.2 us)
Async XLA Ops:
  7.2 78.8 %copy-start = (bf16[512,2048]{1,0:T(8,128)(2,1)S(1)}, bf16[512,2048]{1,0:T(8,128)(2,1)}, u32[]{:S(2)}) copy-start(bf16[512,2048]{1,0:T(8,128)(2,1)} %param.15) | copy-start | bytes 6291460
  7.2 41.5 %copy-start.21 = (s32[1,4]{1,0:T(1,128)S(1)}, s32[1,4]{1,0:T(1,128)}, u32[]{:S(2)}) copy-start(s32[1,4]{1,0:T(1,128)} %param.12) | copy-start | bytes 52
  7.2 41.7 %copy-start.4 = (bf16[512,512]{1,0:T(8,128)(2,1)S(1)}, bf16[512,512]{1,0:T(8,128)(2,1)}, u32[]{:S(2)}) copy-start(bf16[512,512]{1,0:T(8,128)(2,1)} %param.17) | copy-start | bytes 1572868
  26.5 23.4 %copy-start.18 = (s32[512,8]{0,1:T(8,128)S(1)}, s32[512,8]{0,1:T(8,128)}, u32[]{:S(2)}) copy-start(s32[512,8]{0,1:T(8,128)} %param.13) | copy-start | bytes 49156
  40.1 43.1 %copy-start.19 = (s32[512]{0:T(512)S(1)}, s32[512]{0:T(512)}, u32[]{:S(2)}) copy-start(s32[512]{0:T(512)} %param.11) | copy-start | bytes 6148
  40.1 25.3 %all-to-all-start.2 = ((bf16[64,4,2,512]{3,2,1,0:T(2,128)(2,1)}), bf16[64,4,2,512]{3,2,1,0:T(2,128)(2,1)S(1)}, u32[]{:S(2)}, u32[]{:S(2)}) async-start(bf16[64,4,2,512]{3,2,1,0:T(2,128)(2,1)} %reshape.215), calls=%async_computation.2 | async-start | bytes 1048576 | tf_op jit(solution)/shard_map/all_to_all | solution.py:80
  66.6 13.5 %all-to-all-start.3 = ((bf16[64,4,2,512]{3,2,0,1:T(2,128)(2,1)}), bf16[64,4,2,512]{3,2,0,1:T(2,128)(2,1)S(1)}, u32[]{:S(2)}, u32[]{:S(2)}) async-start(bf16[64,4,2,512]{3,2,0,1:T(2,128)(2,1)} %copy.146), calls=%async_computation.3 | async-start | bytes 1048576 | tf_op jit(solution)/shard_map/all_to_all | solution.py:79
  70.0 349.4 %all-reduce.7.cloned.1.call-start = ((), (), s32[]{:S(2)}) async-start(), calls=%async_computation.6 | async-start | bytes 11534336 | tf_op jit(solution)/shard_map/psum | solution.py:119
  85.5 0.5 copy-start.16
  89.9 1.4 copy-start.7
  96.5 4.9 %copy-start.8 = (bf16[64,4,8,128]{3,2,1,0:T(8,128)(2,1)S(1)}, bf16[64,4,8,128]{3,2,1,0:T(8,128)(2,1)}, u32[]{:S(2)}) copy-start(bf16[64,4,8,128]{3,2,1,0:T(8,128)(2,1)} %get-tuple-element.46) | copy-start | bytes 1572868
  101.3 2.6 copy-start.2
  102.2 1.0 copy-start.1
  115.3 5.1 %copy-start.10 = (bf16[512,512]{0,1:T(8,128)(2,1)S(1)}, bf16[512,512]{0,1:T(8,128)(2,1)}, u32[]{:S(2)}) copy-start(bf16[512,512]{0,1:T(8,128)(2,1)} %copy.176) | copy-start | bytes 1572868
  115.3 6.3 %copy-start.11 = (bf16[512,512]{0,1:T(8,128)(2,1)S(1)}, bf16[512,512]{0,1:T(8,128)(2,1)}, u32[]{:S(2)}) copy-start(bf16[512,512]{0,1:T(8,128)(2,1)} %copy.177) | copy-start | bytes 1572868
  120.4 2.9 copy-start.3
  120.4 2.9 copy-start.13
  137.8 1.3 copy-start.17
  137.8 1.6 copy-start.9
  137.8 4.0 copy-start.5
  139.8 0.8 copy-start.12
  141.8 1.5 copy-start.20
  143.3 35.9 %copy-start.6 = (bf16[512,512]{1,0:T(8,128)(2,1)S(1)}, bf16[512,512]{1,0:T(8,128)(2,1)}, u32[]{:S(2)}) copy-start(bf16[512,512]{1,0:T(8,128)(2,1)} %get-tuple-element.45) | copy-start | bytes 1572868
  147.9 24.7 %all-to-all-start.4 = ((bf16[64,4,2,512]{3,2,1,0:T(2,128)(2,1)}), bf16[64,4,2,512]{3,2,1,0:T(2,128)(2,1)}, u32[]{:S(2)}, u32[]{:S(2)}) async-start(bf16[64,4,2,512]{3,2,1,0:T(2,128)(2,1)} %reshape.212), calls=%async_computation.4 | async-start | bytes 1048576 | tf_op jit(solution)/shard_map/all_to_all | solution.py:91
  174.8 14.1 %all-to-all-start.5 = ((bf16[64,4,2,512]{3,2,0,1:T(2,128)(2,1)}), bf16[64,4,2,512]{3,2,0,1:T(2,128)(2,1)}, u32[]{:S(2)}, u32[]{:S(2)}) async-start(bf16[64,4,2,512]{3,2,0,1:T(2,128)(2,1)} %copy.164), calls=%async_computation.5 | async-start | bytes 1048576 | tf_op jit(solution)/shard_map/all_to_all | solution.py:90
  419.4 4.9 %copy-start.14 = (f32[512,512]{1,0:T(8,128)S(1)}, f32[512,512]{1,0:T(8,128)}, u32[]{:S(2)}) copy-start(f32[512,512]{1,0:T(8,128)} %get-tuple-element.42) | copy-start | bytes 3145732
  419.4 6.0 %copy-start.15 = (f32[256,512]{1,0:T(8,128)S(1)}, f32[256,512]{1,0:T(8,128)}, u32[]{:S(2)}) copy-start(f32[256,512]{1,0:T(8,128)} %get-tuple-element.40) | copy-start | bytes 1572868
Sparse Core Ops, SparseCore 0:
  143.4 275.9 all-reduce.6
where the time goes:
time: 434 us; the launch traced here: 433 us
  waiting for transfers between devices  267 us (62%)
  local copies, waits for them, and re-layouts  40.3 us (9%)
  matrix products  37.4 us (9%)
  blocking collectives  26.2 us (6%)
  other arithmetic  24 us (6%)
  starting transfers between devices  23.4 us (5%)
  between operations  14.4 us (3%)
    psum x1, waiting for transfers between devices, on_device(): lax.psum((d_leaf.astype(jnp.float32), d_in.astype(jnp.float32), d_out.ast...  222 us
    all_to_all x1, blocking collectives, send_asked(): lax.all_to_all(wanted, 'dp', split_axis=0, concat_axis=0, tiled=True)  18.3 us
    all_to_all x1, waiting for transfers between devices, send_returned(): lax.all_to_all(gradients, 'dp', split_axis=0, concat_axis=0, tiled=True)  17.6 us
    all_to_all x1, waiting for transfers between devices, send_fetched(): lax.all_to_all(fetched, 'dp', split_axis=0, concat_axis=0, tiled=True)  15.3 us
  transfers between devices with their start and end apart: 5, of which 5 were waited for; matrix products, arithmetic and copies ran while one was open for 6% of the time, Pallas kernels for 0%

commit v1 on v0

--- a/solution.py
+++ b/solution.py
@@ -117,8 +117,10 @@
     d_rows, d_leaf, d_in = pull_front((d_inputs, d_gated))
     returned = send_returned(d_rows.reshape(data_count, replica_count, -1, width))
     leaf_sum, in_sum, out_sum = lax.psum(
-        (d_leaf.astype(jnp.float32), d_in.astype(jnp.float32), d_out.astype(jnp.float32)),
-        ("dp", "rep"),
+        lax.psum(
+            (d_leaf.astype(jnp.float32), d_in.astype(jnp.float32), d_out.astype(jnp.float32)), "dp"
+        ),
+        "rep",
     )
     table_grad = (
         jnp.zeros(item_table.shape, jnp.float32)

time: 434 us -> 488 us (1.12)
  waiting for transfers between devices: 267 us -> 316 us
    psum x0 -> x1, waiting for transfers between devices: none -> 70 us  [on_device(): lax.psum(lax.psum((d_leaf.astype(jnp.float32), d_in.astype(jnp.float32),...]
    psum x1, waiting for transfers between devices: 222 us -> 196 us  [on_device(): lax.psum((d_leaf.astype(jnp.float32), d_in.astype(jnp.float32), d_out.ast...]
    all_to_all x1, waiting for transfers between devices: 5.33 us -> 11.2 us  [send_returned(): lax.all_to_all(lax.all_to_all(gradients, 'dp', split_axis=0, concat_axis=...]
  transfers between devices with their start and end apart: 5 -> 6, of which waited for: 5 -> 6; matrix products, arithmetic and copies ran while one was open for 6% -> 5% of each run, Pallas kernels for 0% -> 0%
where the time goes in v1:
time: 488 us; the launch traced here: 485 us
  waiting for transfers between devices  316 us (65%)
  local copies, waits for them, and re-layouts  43.3 us (9%)
  matrix products  37.4 us (8%)
  blocking collectives  26.2 us (5%)
  starting transfers between devices  24 us (5%)
  other arithmetic  23.4 us (5%)
  between operations  14.4 us (3%)
    psum x1, waiting for transfers between devices, on_device(): lax.psum((d_leaf.astype(jnp.float32), d_in.astype(jnp.float32), d_out.ast...  196 us
    psum x1, waiting for transfers between devices, on_device(): lax.psum(lax.psum((d_leaf.astype(jnp.float32), d_in.astype(jnp.float32),...  70 us
    all_to_all x1, blocking collectives, send_asked(): lax.all_to_all(wanted, 'dp', split_axis=0, concat_axis=0, tiled=True)  18.3 us
    all_to_all x1, waiting for transfers between devices, send_returned(): lax.all_to_all(gradients, 'dp', split_axis=0, concat_axis=0, tiled=True)  16.3 us
    all_to_all x1, waiting for transfers between devices, send_fetched(): lax.all_to_all(fetched, 'dp', split_axis=0, concat_axis=0, tiled=True)  15.3 us
    all_to_all x1, waiting for transfers between devices, send_returned(): lax.all_to_all(lax.all_to_all(gradients, 'dp', split_axis=0, concat_axis=...  11.2 us
  transfers between devices with their start and end apart: 6, of which 6 were waited for; matrix products, arithmetic and copies ran while one was open for 5% of the time, Pallas kernels for 0%

profile of v1, /device:TPU:97, one launch (start us, length us, event | category | flops | bytes accessed | tf_op | source)
XLA Modules:
  0.0 484.9 jit_solution(11517831942194785652)
XLA Ops:
  8.2 18.3 %all_to_all.30 = s32[64,4,2]{1,2,0:T(2,128)S(1)} all-to-all(s32[64,4,2]{1,2,0:T(2,128)S(1)} %copy.143), channel_id=1, replica_groups=mesh['dp'=64,'rep'=4] {'dp'}, dimensions={0} | all-to-all | bytes 4096 | tf_op jit(solution)/shard_map/all_to_all | solution.py:69
  26.7 7.9 %all_to_all.31 = s32[4,1,128]{2,1,0:T(1,128)S(1)} all-to-all(s32[4,1,128]{2,1,0:T(1,128)S(1)} %reshape.234), channel_id=1, replica_groups=mesh['dp'=64,'rep'=4] {'rep'}, dimensions={0} | all-to-all | bytes 4096 | tf_op jit(solution)/shard_map/all_to_all | solution.py:68
  36.2 3.6 gather_fusion
  41.8 8.5 %all-to-all-start.2 = ((bf16[64,4,2,512]{3,2,1,0:T(2,128)(2,1)}), bf16[64,4,2,512]{3,2,1,0:T(2,128)(2,1)S(1)}, u32[]{:S(2)}, u32[]{:S(2)}) async-start(bf16[64,4,2,512]{3,2,1,0:T(2,128)(2,1)} %reshape.215), calls=%async_computation.2 | async-start | bytes 1048576 | tf_op jit(solution)/shard_map/all_to_all | solution.py:80
  51.8 15.3 %all-to-all-done.2 = bf16[64,4,2,512]{3,2,1,0:T(2,128)(2,1)S(1)} async-done(((bf16[64,4,2,512]{3,2,1,0:T(2,128)(2,1)}), bf16[64,4,2,512]{3,2,1,0:T(2,128)(2,1)S(1)}, u32[]{:S(2)}, u32[]{:S(2)}) %all-to-all-start.2) | async-done | bytes 524320 | tf_op jit(solution)/shard_map/all_to_all | solution.py:80
  68.3 3.5 all-to-all-start.3
  72.2 2.3 fusion.42
  74.5 7.3 %all-to-all-done.3 = bf16[64,4,2,512]{3,2,0,1:T(2,128)(2,1)S(1)} async-done(((bf16[64,4,2,512]{3,2,0,1:T(2,128)(2,1)}), bf16[64,4,2,512]{3,2,0,1:T(2,128)(2,1)S(1)}, u32[]{:S(2)}, u32[]{:S(2)}) %all-to-all-start.3) | async-done | bytes 524320 | tf_op jit(solution)/shard_map/all_to_all | solution.py:79
  87.8 3.8 multiply_convert_fusion
  94.1 2.1 copy.176
  98.3 4.9 %select_convert_fusion = (bf16[4,512,512]{2,1,0:T(8,128)(2,1)S(1)}, f32[4,512,512]{2,1,0:T(8,128)}) fusion(pred[512,512]{1,0:T(8,128)(4,1)S(1)} %fusion.22, bf16[512,4,128]{0,2,1:T(8,128)(2,1)} %bitcast.68, bf16[512,4,128]{0,2,1:T(8,128)(2,1)} %bitcast.70), kind=kOutput, calls=%fused_computation.11 | convolution fusion | flops 275775488 | bytes 7602176 | tf_op jit(solution)/shard_map/jvp(qhd,khd->hqk)/dot_general | solution.py:49
  105.7 2.6 copy.171
  108.3 2.1 multiply_reduce_fusion
  111.1 3.0 fusion.40
  115.0 2.1 copy.172
  117.1 5.1 %fusion.4 = bf16[4,512,512]{2,1,0:T(8,128)(2,1)S(1)} fusion(f32[4,512,512]{2,1,0:T(8,128)} %get-tuple-element.60, pred[512,512]{1,0:T(8,128)(4,1)S(1)} %fusion.22, bf16[4,128,512]{2,1,0:T(8,128)(2,1)} %bitcast.72, bf16[64,4,8,128]{3,2,1,0:T(8,128)(2,1)} %get-tuple-element.49), kind=kOutput, calls=%fused_computation.10 | convolution fusion | flops 283115520 | bytes 7602176 | tf_op jit(solution)/shard_map/transpose(jvp(hqk,khd->qhd))/dot_general | solution.py:54
  126.5 2.1 copy.173
  130.6 2.1 copy.175
  132.7 3.6 fusion
  136.3 3.3 fusion.5
  145.1 196.2 %all-reduce.9.cloned.1.call-done = (f32[256,512]{1,0:T(8,128)}, f32[512,2048]{1,0:T(8,128)}, f32[512,512]{1,0:T(8,128)}) async-done(((f32[256,512]{1,0:T(8,128)}, f32[512,2048]{1,0:T(8,128)}, f32[512,512]{1,0:T(8,128)}), (f32[256,512]{1,0:T(8,128)}, f32[512,2048]{1,0:T(8,128)}, f32[512,512]{1,0:T(8,128)})) %all-reduce.9.cloned.1.call-update) | async-done | bytes 5767184 | tf_op jit(solution)/shard_map/psum | solution.py:120
  341.3 2.5 convolution_convert_fusion.1
  345.9 7.3 %all-to-all-start.4 = ((bf16[64,4,2,512]{3,2,1,0:T(2,128)(2,1)}), bf16[64,4,2,512]{3,2,1,0:T(2,128)(2,1)}, u32[]{:S(2)}, u32[]{:S(2)}) async-start(bf16[64,4,2,512]{3,2,1,0:T(2,128)(2,1)} %reshape.212), calls=%async_computation.4 | async-start | bytes 1048576 | tf_op jit(solution)/shard_map/all_to_all | solution.py:91
  353.5 16.3 %all-to-all-done.4 = bf16[64,4,2,512]{3,2,1,0:T(2,128)(2,1)} async-done(((bf16[64,4,2,512]{3,2,1,0:T(2,128)(2,1)}), bf16[64,4,2,512]{3,2,1,0:T(2,128)(2,1)}, u32[]{:S(2)}, u32[]{:S(2)}) %all-to-all-start.4) | async-done | bytes 524320 | tf_op jit(solution)/shard_map/all_to_all | solution.py:91
  369.9 2.2 copy.164
  372.1 4.4 all-to-all-start.5
  376.5 2.3 fusion.11
  378.9 2.0 copy.167
  380.9 11.2 %all-to-all-done.5 = bf16[64,4,2,512]{3,2,0,1:T(2,128)(2,1)} async-done(((bf16[64,4,2,512]{3,2,0,1:T(2,128)(2,1)}), bf16[64,4,2,512]{3,2,0,1:T(2,128)(2,1)}, u32[]{:S(2)}, u32[]{:S(2)}) %all-to-all-start.5) | async-done | bytes 524320 | tf_op jit(solution)/shard_map/all_to_all | solution.py:90
  397.0 4.2 scatter_custom_fusion
  401.3 70.0 %all-reduce.11.cloned.1.call-done = (f32[256,512]{1,0:T(8,128)}, f32[512,2048]{1,0:T(8,128)}, f32[512,512]{1,0:T(8,128)}) async-done(((f32[256,512]{1,0:T(8,128)}, f32[512,2048]{1,0:T(8,128)}, f32[512,512]{1,0:T(8,128)}), (f32[256,512]{1,0:T(8,128)}, f32[512,2048]{1,0:T(8,128)}, f32[512,512]{1,0:T(8,128)})) %all-reduce.11.cloned.1.call-update) | async-done | bytes 5767184 | tf_op jit(solution)/shard_map/psum | solution.py:119
  471.3 4.9 %broadcast_multiply_fusion = f32[512,2048]{1,0:T(8,128)} fusion(f32[512,2048]{1,0:T(8,128)} %get-tuple-element.44), kind=kLoop, calls=%fused_computation.17 | loop fusion | flops 1048576 | bytes 8388608 | tf_op jit(solution)/shard_map/mul | solution.py:131
  (102 shorter events, 43.6 us)
Async XLA Ops:
  7.2 80.6 %copy-start = (bf16[512,2048]{1,0:T(8,128)(2,1)S(1)}, bf16[512,2048]{1,0:T(8,128)(2,1)}, u32[]{:S(2)}) copy-start(bf16[512,2048]{1,0:T(8,128)(2,1)} %param.15) | copy-start | bytes 6291460
  7.2 43.2 %copy-start.21 = (s32[1,4]{1,0:T(1,128)S(1)}, s32[1,4]{1,0:T(1,128)}, u32[]{:S(2)}) copy-start(s32[1,4]{1,0:T(1,128)} %param.12) | copy-start | bytes 52
  7.2 43.4 %copy-start.4 = (bf16[512,512]{1,0:T(8,128)(2,1)S(1)}, bf16[512,512]{1,0:T(8,128)(2,1)}, u32[]{:S(2)}) copy-start(bf16[512,512]{1,0:T(8,128)(2,1)} %param.17) | copy-start | bytes 1572868
  26.5 25.1 %copy-start.18 = (s32[512,8]{0,1:T(8,128)S(1)}, s32[512,8]{0,1:T(8,128)}, u32[]{:S(2)}) copy-start(s32[512,8]{0,1:T(8,128)} %param.13) | copy-start | bytes 49156
  41.8 43.1 %copy-start.19 = (s32[512]{0:T(512)S(1)}, s32[512]{0:T(512)}, u32[]{:S(2)}) copy-start(s32[512]{0:T(512)} %param.11) | copy-start | bytes 6148
  41.8 25.3 %all-to-all-start.2 = ((bf16[64,4,2,512]{3,2,1,0:T(2,128)(2,1)}), bf16[64,4,2,512]{3,2,1,0:T(2,128)(2,1)S(1)}, u32[]{:S(2)}, u32[]{:S(2)}) async-start(bf16[64,4,2,512]{3,2,1,0:T(2,128)(2,1)} %reshape.215), calls=%async_computation.2 | async-start | bytes 1048576 | tf_op jit(solution)/shard_map/all_to_all | solution.py:80
  68.3 13.5 %all-to-all-start.3 = ((bf16[64,4,2,512]{3,2,0,1:T(2,128)(2,1)}), bf16[64,4,2,512]{3,2,0,1:T(2,128)(2,1)S(1)}, u32[]{:S(2)}, u32[]{:S(2)}) async-start(bf16[64,4,2,512]{3,2,0,1:T(2,128)(2,1)} %copy.146), calls=%async_computation.3 | async-start | bytes 1048576 | tf_op jit(solution)/shard_map/all_to_all | solution.py:79
  71.7 269.6 %all-reduce.9.cloned.1.call-start = ((), (), s32[]{:S(2)}) async-start(), calls=%async_computation.6 | async-start | bytes 11534336 | tf_op jit(solution)/shard_map/psum | solution.py:120
  87.2 0.6 copy-start.16
  91.6 1.4 copy-start.7
  98.3 4.9 %copy-start.8 = (bf16[64,4,8,128]{3,2,1,0:T(8,128)(2,1)S(1)}, bf16[64,4,8,128]{3,2,1,0:T(8,128)(2,1)}, u32[]{:S(2)}) copy-start(bf16[64,4,8,128]{3,2,1,0:T(8,128)(2,1)} %get-tuple-element.49) | copy-start | bytes 1572868
  103.1 2.6 copy-start.2
  104.0 1.0 copy-start.1
  117.1 5.1 %copy-start.10 = (bf16[512,512]{0,1:T(8,128)(2,1)S(1)}, bf16[512,512]{0,1:T(8,128)(2,1)}, u32[]{:S(2)}) copy-start(bf16[512,512]{0,1:T(8,128)(2,1)} %copy.176) | copy-start | bytes 1572868
  117.1 6.3 %copy-start.11 = (bf16[512,512]{0,1:T(8,128)(2,1)S(1)}, bf16[512,512]{0,1:T(8,128)(2,1)}, u32[]{:S(2)}) copy-start(bf16[512,512]{0,1:T(8,128)(2,1)} %copy.177) | copy-start | bytes 1572868
  122.1 2.9 copy-start.3
  122.2 2.9 copy-start.13
  139.6 1.3 copy-start.17
  139.6 1.6 copy-start.9
  139.6 3.9 copy-start.5
  141.6 0.8 copy-start.12
  145.0 196.3 %copy-start.20 = (s32[512]{0:T(512)S(1)}, s32[512]{0:T(512)}, u32[]{:S(2)}) copy-start(s32[512]{0:T(512)} %param.11) | copy-start | bytes 6148
  145.0 326.2 %all-reduce.11.cloned.1.call-start = ((), (), s32[]{:S(2)}) async-start(), calls=%async_computation.7 | async-start | bytes 11534336 | tf_op jit(solution)/shard_map/psum | solution.py:119
  341.3 35.2 %copy-start.6 = (bf16[512,512]{1,0:T(8,128)(2,1)S(1)}, bf16[512,512]{1,0:T(8,128)(2,1)}, u32[]{:S(2)}) copy-start(bf16[512,512]{1,0:T(8,128)(2,1)} %get-tuple-element.48) | copy-start | bytes 1572868
  345.9 24.0 %all-to-all-start.4 = ((bf16[64,4,2,512]{3,2,1,0:T(2,128)(2,1)}), bf16[64,4,2,512]{3,2,1,0:T(2,128)(2,1)}, u32[]{:S(2)}, u32[]{:S(2)}) async-start(bf16[64,4,2,512]{3,2,1,0:T(2,128)(2,1)} %reshape.212), calls=%async_computation.4 | async-start | bytes 1048576 | tf_op jit(solution)/shard_map/all_to_all | solution.py:91
  372.1 20.0 %all-to-all-start.5 = ((bf16[64,4,2,512]{3,2,0,1:T(2,128)(2,1)}), bf16[64,4,2,512]{3,2,0,1:T(2,128)(2,1)}, u32[]{:S(2)}, u32[]{:S(2)}) async-start(bf16[64,4,2,512]{3,2,0,1:T(2,128)(2,1)} %copy.164), calls=%async_computation.5 | async-start | bytes 1048576 | tf_op jit(solution)/shard_map/all_to_all | solution.py:90
  471.3 4.9 %copy-start.14 = (f32[512,512]{1,0:T(8,128)S(1)}, f32[512,512]{1,0:T(8,128)}, u32[]{:S(2)}) copy-start(f32[512,512]{1,0:T(8,128)} %get-tuple-element.45) | copy-start | bytes 3145732
  471.3 6.0 %copy-start.15 = (f32[256,512]{1,0:T(8,128)S(1)}, f32[256,512]{1,0:T(8,128)}, u32[]{:S(2)}) copy-start(f32[256,512]{1,0:T(8,128)} %get-tuple-element.43) | copy-start | bytes 1572868
Sparse Core Ops, SparseCore 0:
  145.2 196.0 all-reduce.8
  344.0 127.2 all-reduce.10
